TPU v7x, 32 devices: a whole 2x2x4 slice. The times are simulated.
32 devices in a mesh: wide: 8 (over z, y), narrow: 4 (over x, core).
Axes of the slice: x: 2, y: 2, z: 4, core: 2. Of those that a mesh axis runs over, the one named last changes fastest.
Arguments:
- features: bfloat16 [131072, 512], P(('wide', 'narrow'))
- coefficients: float32 [131072, 128], P(('wide', 'narrow')), may hold values from -0.12 to 0.12
- targets: bfloat16 [131072, 128], P(('wide', 'narrow')), may hold values from -6 to 6
- block_rows: int32 [2, 512], replicated, may hold values from 0 to 4095, as said below
- block_owner: int32 [2], replicated, may hold values from 0 to 31, as said below
Outputs:
- new_coefficients: float32 [131072, 128], P(('wide', 'narrow'))
Inputs may be any that keep to these rules, and one draw needn't show every extreme that they name: `block_rows`: each row lists 512 distinct local rows of the shard of device block_owner[i]. `block_owner`: the 2 owners are distinct and one of them is the last device; device number d holds samples d * 4096 to (d + 1) * 4096 - 1, d being its wide index times the narrow axis's size plus its narrow index.
All inputs are finite; a program needn't handle non-finite values.
Results may differ from a plain program's by a relative error of at most 0.0023.
Values may be sent and summed in bfloat16 or wider, within the bound.
A program may use at most 64 MiB of HBM per device.

v0:
```python
import jax
import jax.numpy as jnp
from jax import lax
from jax.sharding import PartitionSpec as P

ridge_term = 0.5


def spread_2(value, axis, source):
    kept = jnp.where(lax.axis_index(axis) == source, value, 0).astype(value.dtype)
    return lax.psum(kept, axis)


def square_sums(feature_rows):
    widened = feature_rows.astype(jnp.float32)
    return jnp.sum(widened * widened, axis=1)


def kernel_values(left_rows, left_squares, right_rows, right_squares):
    products = lax.dot_general(
        left_rows, right_rows, (((1,), (1,)), ((), ())), preferred_element_type=jnp.float32
    )
    distance = left_squares[:, None] + right_squares[None, :] - 2.0 * products
    return jnp.exp(-distance / left_rows.shape[1])


def cholesky_solve(block_feats, block_squares, right_side):
    gram_matrix = kernel_values(block_feats, block_squares, block_feats, block_squares)
    gram_matrix = gram_matrix + ridge_term * jnp.eye(block_feats.shape[0], dtype=jnp.float32)
    factor = jnp.linalg.cholesky(gram_matrix)
    lower_part = lax.linalg.triangular_solve(factor, right_side, left_side=True, lower=True)
    return lax.linalg.triangular_solve(
        factor, lower_part, left_side=True, lower=True, transpose_a=True
    )


def per_device(features, coefficients, targets, block_rows, block_owner):
    iterations = block_rows.shape[0]
    feat_count = features.shape[1]
    narrow_count = lax.axis_size("narrow")
    device = lax.axis_index("wide") * narrow_count + lax.axis_index("narrow")
    local_squares = square_sums(features)
    updated = coefficients
    blocks = []
    local_terms = []
    for iteration in range(iterations):
        sample_rows = block_rows[iteration]
        holder = block_owner[iteration]
        joined = jnp.concatenate(
            [features[sample_rows], coefficients[sample_rows].astype(jnp.bfloat16)], axis=1
        )
        arrived = spread_2(joined, ("wide", "narrow"), holder)
        block_feats = arrived[:, :feat_count]
        stale_rows = arrived[:, feat_count:]
        block_squares = square_sums(block_feats)
        blocks.append((block_feats, block_squares, stale_rows))
        is_holder = device == holder
        masked = jnp.where(is_holder, coefficients.at[sample_rows].set(0.0), coefficients).astype(
            jnp.bfloat16
        )
        kernel = kernel_values(block_feats, block_squares, features, local_squares).astype(
            jnp.bfloat16
        )
        product = jnp.dot(kernel, masked, preferred_element_type=jnp.float32)
        own_targets = jnp.where(is_holder, targets[sample_rows].astype(jnp.float32), 0.0)
        local_terms.append(own_targets - product)
    reduce_local_terms = jnp.stack(local_terms)
    right_sides = lax.psum(reduce_local_terms, ("wide", "narrow"))
    solutions = []
    for iteration in range(iterations):
        block_feats, block_squares, stale_rows = blocks[iteration]
        target = right_sides[iteration]
        for earlier in range(iteration):
            between = kernel_values(
                block_feats, block_squares, blocks[earlier][0], blocks[earlier][1]
            ).astype(jnp.bfloat16)
            fresh_rows = solutions[earlier].astype(jnp.bfloat16)
            fresh_part = jnp.dot(between, fresh_rows, preferred_element_type=jnp.float32)
            stale_part = jnp.dot(between, blocks[earlier][2], preferred_element_type=jnp.float32)
            target = target - (fresh_part - stale_part)
        solutions.append(cholesky_solve(block_feats, block_squares, target))
    solved = jnp.stack(solutions)
    for iteration in range(iterations):
        sample_rows = block_rows[iteration]
        holder = block_owner[iteration]
        updated = jnp.where(
            device == holder, updated.at[sample_rows].set(solved[iteration]), updated
        )
    return updated


def solution(mesh):
    placed = (
        P(("wide", "narrow"), None),
        P(("wide", "narrow"), None),
        P(("wide", "narrow"), None),
        P(),
        P(),
    )
    return jax.shard_map(
        per_device,
        mesh=mesh,
        in_specs=placed,
        out_specs=P(("wide", "narrow"), None),
        check_vma=False,
    )
```

profile of v0, /device:TPU:0, one launch (start us, length us, event | category | flops | bytes accessed | tf_op | source)
XLA Modules:
  0.0 506.2 jit_solution(14191106905419013107)
XLA Ops:
  7.4 5.5 %gather_fusion = bf16[512,512]{1,0:T(8,128)(2,1)} fusion(bf16[4096,512]{1,0:T(8,128)(2,1)} %param.10, s32[1024]{0:T(1024)S(1)} %pad_clamp_fusion.1), kind=kCustom, calls=%fused_computation | custom fusion | bytes 1050624 | tf_op jit(solution)/shard_map/gather | solution.py:50
  14.0 5.4 %gather_fusion.4 = bf16[512,512]{1,0:T(8,128)(2,1)} fusion(bf16[4096,512]{1,0:T(8,128)(2,1)} %param.10, s32[1024]{0:T(1024)S(1)} %pad_clamp_fusion), kind=kCustom, calls=%fused_computation.4 | custom fusion | bytes 1050624 | tf_op jit(solution)/shard_map/gather | solution.py:50
  42.4 118.5 %all-reduce.7.cloned.1.call-done = (bf16[512,640]{1,0:T(8,128)(2,1)}, bf16[512,640]{1,0:T(8,128)(2,1)}) async-done(((bf16[512,640]{1,0:T(8,128)(2,1)}, bf16[512,640]{1,0:T(8,128)(2,1)}), (bf16[512,640]{1,0:T(8,128)(2,1)}, bf16[512,640]{1,0:T(8,128)(2,1)})) %all-reduce.7.cloned.1.call-update) | async-done | bytes 1310736 | tf_op jit(solution)/shard_map/psum | solution.py:11
  166.9 5.9 %fusion.19 = f32[1,512,128]{2,1,0:T(8,128)S(1)} fusion(bf16[4096,512]{1,0:T(8,128)(2,1)} %param.10, f32[4096]{0:T(1024)S(1)} %multiply_reduce_fusion, f32[512]{0:T(512)} %copy-done.29, f32[4096,128]{1,0:T(8,128)} %scatter_custom_fusion, f32[4096,128]{1,0:T(8,128)S(1)} %copy-done.2, pred[]{:T(512)S(6)} %eq.17, bf16[512,640]{1,0:T(8,128)(2,1)} %get-tuple-element.56, ...), kind=kOutput, calls=%fused_computation.46 | convolution fusion | flops 2697658368 | bytes 9325568 | tf_op jit(solution)/shard_map/dot_general | solution.py:64
  172.8 6.6 %fusion.17 = f32[1,512,128]{2,1,0:T(8,128)} fusion(bf16[4096,512]{1,0:T(8,128)(2,1)} %param.10, f32[512]{0:T(512)} %copy-done.27, f32[4096]{0:T(1024)S(1)} %multiply_reduce_fusion, f32[4096,128]{1,0:T(8,128)} %copy-done.3, f32[4096,128]{1,0:T(8,128)S(1)} %copy-done.2, pred[]{:T(512)S(6)} %eq.16, bf16[512,640]{1,0:T(8,128)(2,1)} %get-tuple-element.57, ...), kind=kOutput, calls=%fused_computation.44 | convolution fusion | flops 2697658368 | bytes 9325568 | tf_op jit(solution)/shard_map/dot_general | solution.py:64
  182.9 11.9 %cholesky.286 = f32[128,128]{1,0:T(8,128)S(1)} custom-call(f32[128,128]{1,0:T(8,128)S(1)} %cholesky.426), custom_call_target="Cholesky" | custom-call | tf_op jit(solution)/shard_map/jit(cholesky)/cholesky | solution.py:30
  195.0 9.8 %custom-call.31 = f32[1,128,128]{1,2,0:T(8,128)S(1)} custom-call(f32[1,128,128]{2,1,0:T(8,128)S(1)} %get-tuple-element.81), custom_call_target="InvertDiagBlocksLowerTriangular" | custom-call | tf_op jit(solution)/shard_map/jit(cholesky)/cholesky | solution.py:30
  207.3 11.7 %cholesky.305 = f32[128,128]{1,0:T(8,128)S(1)} custom-call(f32[128,128]{1,0:T(8,128)S(1)} %cholesky.430), custom_call_target="Cholesky" | custom-call | tf_op jit(solution)/shard_map/jit(cholesky)/cholesky | solution.py:30
  220.4 9.8 %custom-call.32 = f32[1,128,128]{1,2,0:T(8,128)S(1)} custom-call(f32[1,128,128]{2,1,0:T(8,128)S(1)} %get-tuple-element.78), custom_call_target="InvertDiagBlocksLowerTriangular" | custom-call | tf_op jit(solution)/shard_map/jit(cholesky)/cholesky | solution.py:30
  231.8 12.1 %cholesky.326 = f32[128,128]{1,0:T(8,128)S(1)} custom-call(f32[128,128]{1,0:T(8,128)S(1)} %cholesky.435), custom_call_target="Cholesky" | custom-call | tf_op jit(solution)/shard_map/jit(cholesky)/cholesky | solution.py:30
  244.6 9.8 %custom-call.33 = f32[1,128,128]{1,2,0:T(8,128)S(1)} custom-call(f32[1,128,128]{2,1,0:T(8,128)S(1)} %get-tuple-element.75), custom_call_target="InvertDiagBlocksLowerTriangular" | custom-call | tf_op jit(solution)/shard_map/jit(cholesky)/cholesky | solution.py:30
  255.8 11.7 %cholesky.343 = f32[128,128]{1,0:T(8,128)S(1)} custom-call(f32[128,128]{1,0:T(8,128)S(1)} %convolution_subtract_fusion.18), custom_call_target="Cholesky" | custom-call | tf_op jit(solution)/shard_map/jit(cholesky)/cholesky | solution.py:30
  270.9 7.6 %while.8 = (s32[]{:T(128)}, f32[512,512]{1,0:T(8,128)S(1)}, s32[4,2]{0,1:T(2,128)S(1)}, f32[4,128,128]{2,1,0:T(8,128)S(1)}, s32[]{:T(128)}) while((s32[]{:T(128)}, f32[512,512]{1,0:T(8,128)S(1)}, s32[4,2]{0,1:T(2,128)S(1)}, f32[4,128,128]{2,1,0:T(8,128)S(1)}, s32[]{:T(128)}) %tuple.61), condition=%wide.while_cond.1, body=%wide.while_body.1.sunk | while | flops 2 | bytes 131181 | solution.py:32
  279.2 40.3 %custom-call.35 = f32[4,128,128]{1,2,0:T(8,128)S(1)} custom-call(f32[4,128,128]{2,1,0:T(8,128)} %copy-done.24), custom_call_target="InvertDiagBlocksLowerTriangular" | custom-call | tf_op jit(solution)/shard_map/triangular_solve/custom-call.8 | solution.py:32
  324.5 11.7 %cholesky.358 = f32[128,128]{1,0:T(8,128)S(1)} custom-call(f32[128,128]{1,0:T(8,128)S(1)} %cholesky.439), custom_call_target="Cholesky" | custom-call | tf_op jit(solution)/shard_map/jit(cholesky)/cholesky | solution.py:30
  336.4 9.8 %custom-call.36 = f32[1,128,128]{1,2,0:T(8,128)S(1)} custom-call(f32[1,128,128]{2,1,0:T(8,128)S(1)} %get-tuple-element.71), custom_call_target="InvertDiagBlocksLowerTriangular" | custom-call | tf_op jit(solution)/shard_map/jit(cholesky)/cholesky | solution.py:30
  349.4 11.7 %cholesky.377 = f32[128,128]{1,0:T(8,128)S(1)} custom-call(f32[128,128]{1,0:T(8,128)S(1)} %cholesky.443), custom_call_target="Cholesky" | custom-call | tf_op jit(solution)/shard_map/jit(cholesky)/cholesky | solution.py:30
  362.4 10.2 %custom-call.37 = f32[1,128,128]{1,2,0:T(8,128)S(1)} custom-call(f32[1,128,128]{2,1,0:T(8,128)S(1)} %get-tuple-element.68), custom_call_target="InvertDiagBlocksLowerTriangular" | custom-call | tf_op jit(solution)/shard_map/jit(cholesky)/cholesky | solution.py:30
  375.7 13.2 %cholesky.398 = f32[128,128]{1,0:T(8,128)} custom-call(f32[128,128]{1,0:T(8,128)} %cholesky.448), custom_call_target="Cholesky" | custom-call | tf_op jit(solution)/shard_map/jit(cholesky)/cholesky | solution.py:30
  391.0 11.3 %custom-call.38 = f32[1,128,128]{1,2,0:T(8,128)} custom-call(f32[1,128,128]{2,1,0:T(8,128)} %get-tuple-element.65), custom_call_target="InvertDiagBlocksLowerTriangular" | custom-call | tf_op jit(solution)/shard_map/jit(cholesky)/cholesky | solution.py:30
  404.6 11.7 %cholesky.415 = f32[128,128]{1,0:T(8,128)S(1)} custom-call(f32[128,128]{1,0:T(8,128)S(1)} %convolution_subtract_fusion.15), custom_call_target="Cholesky" | custom-call | tf_op jit(solution)/shard_map/jit(cholesky)/cholesky | solution.py:30
  420.7 11.5 %while.9 = (s32[]{:T(128)}, f32[512,512]{1,0:T(8,128)}, s32[4,2]{0,1:T(2,128)S(1)}, f32[4,128,128]{2,1,0:T(8,128)S(1)}, s32[]{:T(128)}) while((s32[]{:T(128)}, f32[512,512]{1,0:T(8,128)}, s32[4,2]{0,1:T(2,128)S(1)}, f32[4,128,128]{2,1,0:T(8,128)S(1)}, s32[]{:T(128)}) %tuple.72), condition=%wide.while_cond.1.clone, body=%wide.while_body.1.clone.sunk | while | flops 2 | bytes 131181 | solution.py:32
  432.2 39.9 %custom-call.40 = f32[4,128,128]{1,2,0:T(8,128)} custom-call(f32[4,128,128]{2,1,0:T(8,128)S(1)} %get-tuple-element.39), custom_call_target="InvertDiagBlocksLowerTriangular" | custom-call | tf_op jit(solution)/shard_map/triangular_solve/custom-call.8 | solution.py:32
  492.8 4.9 scatter_custom_fusion.3
  (195 shorter events, 102.0 us)
Async XLA Ops:
  6.5 21.3 %copy-start = (bf16[4096,128]{1,0:T(8,128)(2,1)S(1)}, bf16[4096,128]{1,0:T(8,128)(2,1)}, u32[]{:S(2)}) copy-start(bf16[4096,128]{1,0:T(8,128)(2,1)} %param.12) | copy-start | bytes 3145732
  6.5 154.3 %all-reduce.7.cloned.1.call-start = ((), (), s32[]{:S(2)}) async-start(), calls=%async_computation.1 | async-start | bytes 2621440 | tf_op jit(solution)/shard_map/psum | solution.py:11
  7.3 23.7 %copy-start.26 = (s32[512,1]{0,1:T(1,128)}, s32[512,1]{0,1:T(1,128)S(1)}, u32[]{:S(2)}) copy-start(s32[512,1]{0,1:T(1,128)S(1)} %get-tuple-element.83) | copy-start | bytes 6148
  7.3 28.5 %copy-start.25 = (s32[512,1]{0,1:T(1,128)}, s32[512,1]{0,1:T(1,128)S(1)}, u32[]{:S(2)}) copy-start(s32[512,1]{0,1:T(1,128)S(1)} %get-tuple-element.82) | copy-start | bytes 6148
  7.4 5.5 %copy-start.1 = (f32[4096,128]{1,0:T(8,128)S(1)}, f32[4096,128]{1,0:T(8,128)}, u32[]{:S(2)}) copy-start(f32[4096,128]{1,0:T(8,128)} %param.11) | copy-start | bytes 6291460
  14.0 6.5 %copy-start.31 = (s32[2]{0:T(128)S(1)}, s32[2]{0:T(128)}, u32[]{:S(2)}) copy-start(s32[2]{0:T(128)} %param.14) | copy-start | bytes 28
  26.4 447.5 %all-reduce.5.cloned.1.call-start = ((), (), s32[]{:S(2)}) async-start(), calls=%async_computation | async-start | bytes 1048576 | tf_op jit(solution)/shard_map/psum | solution.py:68
  31.1 4.8 copy-start.4
  38.5 3.9 copy-start.3
  162.3 2.9 copy-start.27
  162.4 2.8 copy-start.29
  162.4 2.8 copy-start.22
  179.4 1.9 copy-start.10
  219.1 51.7 %copy-start.32 = (s32[4]{0:T(128)S(1)}, s32[4]{0:T(128)}, u32[]{:S(2)}) copy-start(s32[4]{0:T(128)} %iota_multiply_fusion) | copy-start | bytes 52
  270.8 51.2 %copy-start.9 = (f32[512,512]{0,1:T(8,128)S(1)}, f32[512,512]{0,1:T(8,128)}, u32[]{:S(2)}) copy-start(f32[512,512]{0,1:T(8,128)} %select_add_fusion) | copy-start | bytes 3145732
  375.1 97.1 %copy-start.28 = (f32[512]{0:T(512)S(1)}, f32[512]{0:T(512)}, u32[]{:S(2)}) copy-start(f32[512]{0:T(512)} %copy-done.27) | copy-start | bytes 6148
  375.1 97.1 %copy-start.30 = (f32[512]{0:T(512)S(1)}, f32[512]{0:T(512)}, u32[]{:S(2)}) copy-start(f32[512]{0:T(512)} %copy-done.29) | copy-start | bytes 6148
  475.7 3.9 copy-start.21
  477.1 3.7 copy-start.13
  477.4 3.7 copy-start.8
  480.9 4.8 copy-start.5
  480.9 4.8 copy-start.15
  480.9 4.8 copy-start.18
  492.8 4.9 copy-start.7
  (11 other events, 11.3 us)
Sparse Core Ops, SparseCore 0:
  26.5 134.2 all-reduce.6
  181.5 128.0 all-reduce.4
where the time goes:
time: 513 us; the launch traced here: 506 us
  other arithmetic  269 us (52%)
  waiting for transfers between devices  119 us (23%)
  local copies, waits for them, and re-layouts  56 us (11%)
  matrix products  41.4 us (8%)
  between operations  20.7 us (4%)
    another operation x30, other arithmetic, cholesky_solve(): factor = jnp.linalg.cholesky(gram_matrix)  163 us
    psum x1, waiting for transfers between devices, spread_2(): return lax.psum(kept, axis)  118 us
    another operation x5, other arithmetic, cholesky_solve(): lax.linalg.triangular_solve(factor, lower_part, left_side=True, lower=Tru...  82.2 us
    another operation x27, local copies, waits for them, and re-layouts, cholesky_solve(): lax.linalg.triangular_solve(factor, lower_part, left_side=True, lower=Tru...  19 us
    another operation x12, matrix products, cholesky_solve(): factor = jnp.linalg.cholesky(gram_matrix)  12.7 us
    dot_general x2, matrix products, per_device(): product = jnp.dot(kernel, masked, preferred_element_type=jnp.float32)  12.6 us
    gather x2, local copies, waits for them, and re-layouts, per_device(): features[sample_rows]  10.9 us
  transfers between devices with their start and end apart: 2, of which 1 were waited for; matrix products, arithmetic and copies ran while one was open for 59% of the time, Pallas kernels for 0%

commit v1 on v0

v1 whole, which is shorter than its diff:
```python
import functools
import math

import jax
import jax.numpy as jnp
from jax import lax
from jax.experimental import pallas as pl
from jax.experimental.pallas import tpu as pltpu
from jax.sharding import PartitionSpec as P

ridge_term = 0.5
newton_steps = 8
f32 = jnp.float32
bf16 = jnp.bfloat16
whole_vmem = pl.BlockSpec(memory_space=pltpu.VMEM)
whole_smem = pl.BlockSpec(memory_space=pltpu.SMEM)


def nn_dot(left, right):
    return jnp.dot(left, right, preferred_element_type=f32)


def nt_dot(left, right):
    return lax.dot_general(left, right, (((1,), (1,)), ((), ())), preferred_element_type=f32)


def tn_dot(left, right):
    return lax.dot_general(left, right, (((0,), (0,)), ((), ())), preferred_element_type=f32)


def halves(value):
    high = value.astype(bf16)
    return high, (value - high.astype(f32)).astype(bf16)


def fine_dot(left, right, dot=nn_dot):
    left_high, left_low = halves(left)
    right_high, right_low = halves(right)
    return dot(left_high, right_high) + (dot(left_high, right_low) + dot(left_low, right_high))


def row_squares(rows):
    widened = rows.astype(f32)
    return jnp.sum(widened * widened, axis=1, keepdims=True)


def lane_squares(rows):
    widened = rows.astype(f32)
    high, low = halves(widened * widened)
    ones = jnp.ones((8, rows.shape[1]), bf16)
    return (nt_dot(ones, high) + nt_dot(ones, low))[0:1]


def gather_kernel(flags, rows_down, rows_across, feats, coefs, targs, spread_out, targ_out, mask0_out, mask1_out,
                  squares_out, feat_total, targ_total):
    step = pl.program_id(0)
    tile = feats.shape[0]
    block = rows_down.shape[0]
    first, second = flags[0], flags[1]
    squares_out[...] = lane_squares(feats[...])
    plain = coefs[...].astype(bf16)

    @pl.when(first + second == 0)
    def _():
        mask0_out[...] = plain
        mask1_out[...] = plain

        @pl.when(step == 0)
        def _():
            spread_out[...] = jnp.zeros_like(spread_out)
            targ_out[...] = jnp.zeros_like(targ_out)

    @pl.when(first + second > 0)
    def _():
        lanes = lax.broadcasted_iota(jnp.int32, (block, tile), 1) + step * tile
        pick = jnp.where(lanes == rows_down[...], 1.0, 0.0).astype(bf16)
        feat_part = nn_dot(pick, feats[...])
        targ_part = nn_dot(pick, targs[...])
        subs = lax.broadcasted_iota(jnp.int32, (tile, block), 0) + step * tile
        place = jnp.where(subs == rows_across[...], 1.0, 0.0).astype(bf16)
        taken = nn_dot(place, jnp.ones((block, coefs.shape[1]), bf16)) > 0.5
        cleared = jnp.where(taken, 0.0, coefs[...]).astype(bf16)
        mask0_out[...] = jnp.where(first > 0, cleared, plain)
        mask1_out[...] = cleared

        @pl.when(step == 0)
        def _():
            feat_total[...] = feat_part
            targ_total[...] = targ_part

        @pl.when(step > 0)
        def _():
            feat_total[...] += feat_part
            targ_total[...] += targ_part

        @pl.when(step == pl.num_programs(0) - 1)
        def _():
            for index, flag in enumerate((first, second)):
                keep = flag > 0
                spread_out[pl.ds(index * block, block), :] = jnp.where(keep, feat_total[...], 0.0).astype(bf16)
                targ_out[pl.ds(index * block, block), :] = jnp.where(keep, targ_total[...], 0.0)


def gather_own(flags, rows, features, coefficients, targets):
    count, width = features.shape
    outs = coefficients.shape[1]
    block = rows.shape[0]
    tile = min(1024, count)
    moving = lambda columns: pl.BlockSpec((tile, columns), lambda i: (i, 0))
    still = lambda shape: pl.BlockSpec(shape, lambda i: (0, 0))
    return pl.pallas_call(
        gather_kernel,
        grid=(count // tile,),
        in_specs=[whole_smem, still((block, 1)), still((1, block)), moving(width), moving(outs), moving(outs)],
        out_specs=[
            still((2 * block, width)), still((2 * block, outs)), moving(outs), moving(outs),
            pl.BlockSpec((1, tile), lambda i: (0, i)),
        ],
        out_shape=[
            jax.ShapeDtypeStruct((2 * block, width), bf16), jax.ShapeDtypeStruct((2 * block, outs), f32),
            jax.ShapeDtypeStruct((count, outs), bf16), jax.ShapeDtypeStruct((count, outs), bf16),
            jax.ShapeDtypeStruct((1, count), f32),
        ],
        scratch_shapes=[pltpu.VMEM((block, width), f32), pltpu.VMEM((block, outs), f32)],
        compiler_params=pltpu.CompilerParams(vmem_limit_bytes=40 << 20),
        name="gather_own",
    )(flags, rows[:, None], rows[None, :], features, coefficients, targets)


def terms_kernel(arrived, feats, squares, mask0, mask1, own, terms_out, offsets):
    step = pl.program_id(0)
    width = feats.shape[1]
    block = arrived.shape[0] // 2
    scale = math.log2(math.e) / width

    @pl.when(step == 0)
    def _():
        offsets[...] = row_squares(arrived[...]) * (-scale)
        terms_out[...] = own[...]

    beside = squares[...] * (-scale)
    piece = block // 2
    for part in range(4):
        span = pl.ds(part * piece, piece)
        products = nt_dot(arrived[span, :], feats[...])
        values = jnp.exp2(products * (2.0 * scale) + offsets[span, :] + beside).astype(bf16)
        mask = mask0 if part < 2 else mask1
        terms_out[span, :] -= nn_dot(values, mask[...])


def local_terms(arrived, features, squares, mask0, mask1, own):
    count, width = features.shape
    outs = own.shape[1]
    tile = min(1024, count)
    moving = lambda columns: pl.BlockSpec((tile, columns), lambda i: (i, 0))
    still = lambda shape: pl.BlockSpec(shape, lambda i: (0, 0))
    return pl.pallas_call(
        terms_kernel,
        grid=(count // tile,),
        in_specs=[
            still(arrived.shape), moving(width), pl.BlockSpec((1, tile), lambda i: (0, i)), moving(outs), moving(outs),
            still(own.shape),
        ],
        out_specs=still(own.shape),
        out_shape=jax.ShapeDtypeStruct(own.shape, f32),
        scratch_shapes=[pltpu.VMEM((arrived.shape[0], 1), f32)],
        compiler_params=pltpu.CompilerParams(vmem_limit_bytes=40 << 20),
        name="local_terms",
    )(arrived, features, squares, mask0, mask1, own)


def newton_plan(size):
    least, most = ridge_term * 0.96, size + ridge_term + 0.1
    radius = (most - least) / (most + least)
    start = 2.0 / (most + least)
    scales = []
    for _ in range(newton_steps):
        scales.append(2.0 / (2.0 - radius * radius))
        radius = radius * radius / (2.0 - radius * radius)
    return start, scales


def invert_pair(matrices, keep):
    size = matrices[0].shape[0]
    start, scales = newton_plan(size)
    eye = jnp.where(
        lax.broadcasted_iota(jnp.int32, (size, size), 0) == lax.broadcasted_iota(jnp.int32, (size, size), 1), 1.0, 0.0
    )
    for index, matrix in enumerate(matrices):
        keep[index] = (2.0 * start * scales[0]) * eye - (start * start * scales[0]) * matrix
    for scale in scales[1:]:
        guesses = [keep[index] for index in range(2)]
        rests = [fine_dot(matrix, guess) for matrix, guess in zip(matrices, guesses)]
        for index in range(2):
            change = fine_dot(guesses[index], rests[index])
            keep[index] = (2.0 * scale) * guesses[index] - scale * change


def factor_kernel(arrived, first_out, cross_out, second_out, between_out):
    width = arrived.shape[1]
    block = arrived.shape[0] // 2
    half = block // 2
    scale = math.log2(math.e) / width

    def values(left, right):
        left_rows, right_rows = arrived[left, :], arrived[right, :]
        distance = row_squares(left_rows) + lane_squares(right_rows) - 2.0 * nt_dot(left_rows, right_rows)
        return jnp.exp2(distance * (-scale))

    span = lambda index, part: pl.ds(index * block + part * half, half)
    ridge = jnp.where(
        lax.broadcasted_iota(jnp.int32, (half, half), 0) == lax.broadcasted_iota(jnp.int32, (half, half), 1),
        ridge_term, 0.0,
    )
    invert_pair([values(span(i, 0), span(i, 0)) + ridge for i in range(2)], first_out)
    rests = []
    for i in range(2):
        low = values(span(i, 1), span(i, 0))
        cross = fine_dot(low, first_out[i])
        cross_out[i] = cross
        rests.append(values(span(i, 1), span(i, 1)) + ridge - fine_dot(cross, low, nt_dot))
    invert_pair(rests, second_out)
    for part in range(2):
        between_out[pl.ds(part * half, half), :] = values(span(1, part), pl.ds(0, block)).astype(bf16)


def factor(arrived):
    block = arrived.shape[0] // 2
    half = block // 2
    shape = jax.ShapeDtypeStruct((2, half, half), f32)
    return pl.pallas_call(
        factor_kernel,
        in_specs=[whole_vmem],
        out_specs=[whole_vmem] * 4,
        out_shape=[shape, shape, shape, jax.ShapeDtypeStruct((block, block), bf16)],
        compiler_params=pltpu.CompilerParams(vmem_limit_bytes=40 << 20),
        name="factor",
    )(arrived)


def finish_kernel(flags, rows_across, coefs, sides, first_inv, cross, second_inv, between, out, pieces):
    step = pl.program_id(0)
    block = rows_across.shape[1]
    half = block // 2
    tile, outs = coefs.shape

    def solve(index, upper, lower):
        rest = lower - fine_dot(cross[index], upper)
        low_part = fine_dot(second_inv[index], rest)
        high_part = fine_dot(first_inv[index], upper) - fine_dot(cross[index], low_part, tn_dot)
        return high_part, low_part

    mine = flags[0] + flags[1] > 0

    @pl.when(mine & (step == 0))
    def _():
        fresh = solve(0, sides[pl.ds(0, half), :], sides[pl.ds(half, half), :])
        sent = jnp.concatenate([part.astype(bf16) for part in fresh], axis=0)
        moved = nn_dot(between[...], sent)
        later = solve(1, sides[pl.ds(block, half), :] - moved[:half], sides[pl.ds(block + half, half), :] - moved[half:])
        for part in range(2):
            value = jnp.where(flags[0] > 0, fresh[part], later[part])
            high = value.astype(bf16)
            rest = value - high.astype(f32)
            mid = rest.astype(bf16)
            low = (rest - mid.astype(f32)).astype(bf16)
            for index, piece in enumerate((high, mid, low)):
                pieces[pl.ds(part * half, half), pl.ds(index * outs, outs)] = piece
        pieces[:, pl.ds(3 * outs, outs)] = jnp.ones((block, outs), bf16)

    @pl.when(mine)
    def _():
        subs = lax.broadcasted_iota(jnp.int32, (tile, block), 0) + step * tile
        place = jnp.where(subs == rows_across[...], 1.0, 0.0).astype(bf16)
        spread = nn_dot(place, pieces[...])
        value = spread[:, :outs] + spread[:, outs : 2 * outs] + spread[:, 2 * outs : 3 * outs]
        out[...] = jnp.where(spread[:, 3 * outs :] > 0.5, value, coefs[...])

    @pl.when(jnp.logical_not(mine))
    def _():
        out[...] = coefs[...]


def finish(flags, rows, coefficients, sides, first_inv, cross, second_inv, between):
    count, outs = coefficients.shape
    block = rows.shape[0]
    tile = min(1024, count)
    moving = pl.BlockSpec((tile, outs), lambda i: (i, 0))
    return pl.pallas_call(
        finish_kernel,
        grid=(count // tile,),
        in_specs=[whole_smem, whole_vmem, moving] + [whole_vmem] * 5,
        out_specs=moving,
        out_shape=jax.ShapeDtypeStruct(coefficients.shape, f32),
        scratch_shapes=[pltpu.VMEM((block, 4 * outs), bf16)],
        compiler_params=pltpu.CompilerParams(vmem_limit_bytes=40 << 20),
        name="finish",
    )(flags, rows[None, :], coefficients, sides, first_inv, cross, second_inv, between)


def per_device(features, coefficients, targets, block_rows, block_owner):
    device = lax.axis_index("wide") * lax.axis_size("narrow") + lax.axis_index("narrow")
    flags = (block_owner == device).astype(jnp.int32)
    rows = jnp.where(flags[0] > 0, block_rows[0], block_rows[1])
    spread, own, mask0, mask1, squares = gather_own(flags, rows, features, coefficients, targets)
    arrived = lax.psum(spread, ("wide", "narrow"))
    terms = local_terms(arrived, features, squares, mask0, mask1, own)
    sides = lax.psum(terms, ("wide", "narrow"))
    parts = factor(arrived)
    return finish(flags, rows, coefficients, sides, *parts)


def solution(mesh):
    rows = P(("wide", "narrow"), None)
    return jax.shard_map(
        per_device,
        mesh=mesh,
        in_specs=(rows, rows, rows, P(), P()),
        out_specs=rows,
        check_vma=False,
    )
```

time: 513 us -> 320 us (0.62)
  other arithmetic: 269 us -> 2.19 us
  waiting for transfers between devices: 119 us -> 249 us
  matrix products: 41.4 us -> 0 us
  local copies, waits for them, and re-layouts: 56 us -> 24 us
  Pallas kernels: 0 us -> 27.2 us
  between operations: 20.7 us -> 13.5 us
    another operation x36 -> x0, other arithmetic: 247 us -> none  [the longest x30 163 us: cholesky_solve(): factor = jnp.linalg.cholesky(gram_matrix)]
    psum x2, waiting for transfers between devices: 118 us -> 249 us  [the longest x1 138 us: per_device(): arrived = lax.psum(spread, ('wide', 'narrow'))]
    pallas_call x0 -> x4, Pallas kernels: none -> 27.2 us  [the longest x1 12.1 us: factor(): pl.pallas_call(factor_kernel, in_specs=[whole_vmem], out_specs=[whole_vme...]
    another operation x40 -> x0, matrix products: 21.1 us -> none  [the longest x12 12.7 us: cholesky_solve(): factor = jnp.linalg.cholesky(gram_matrix)]
    dot_general x7 -> x0, matrix products: 20.2 us -> none  [the longest x2 12.6 us: per_device(): product = jnp.dot(kernel, masked, preferred_element_type=jnp.float32)]
    another operation x35 -> x0, local copies, waits for them, and re-layouts: 19.9 us -> none  [the longest x27 19 us: cholesky_solve(): lax.linalg.triangular_solve(factor, lower_part, left_side=True, lower=Tru...]
    gather x6 -> x0, local copies, waits for them, and re-layouts: 16.2 us -> none  [the longest x2 10.9 us: per_device(): features[sample_rows]]
    unnamed x68 -> x46, local copies, waits for them, and re-layouts: 7.93 us -> 23.8 us
  transfers between devices with their start and end apart: 2 -> 2, of which waited for: 1 -> 2; matrix products, arithmetic and copies ran while one was open for 59% -> 0% of each run, Pallas kernels for 0% -> 4%
where the time goes in v1:
time: 320 us; the launch traced here: 316 us
  waiting for transfers between devices  249 us (78%)
  Pallas kernels  27.2 us (8%)
  local copies, waits for them, and re-layouts  24 us (8%)
  between operations  13.5 us (4%)
    psum x1, waiting for transfers between devices, per_device(): arrived = lax.psum(spread, ('wide', 'narrow'))  138 us
    psum x1, waiting for transfers between devices, per_device(): sides = lax.psum(terms, ('wide', 'narrow'))  112 us
    unnamed x46, local copies, waits for them, and re-layouts  23.8 us
    pallas_call x1, Pallas kernels, factor(): pl.pallas_call(factor_kernel, in_specs=[whole_vmem], out_specs=[whole_vme...  12.1 us
    pallas_call x1, Pallas kernels, local_terms(): pl.pallas_call(terms_kernel, grid=(count // tile,), in_specs=[still(arriv...  8.02 us
  transfers between devices with their start and end apart: 2, of which 2 were waited for; matrix products, arithmetic and copies ran while one was open for 0% of the time, Pallas kernels for 4%

profile of v1, /device:TPU:0, one launch (start us, length us, event | category | flops | bytes accessed | tf_op | source)
XLA Modules:
  0.0 316.4 jit_solution(14731008737318036696)
XLA Ops:
  8.9 2.2 copy-done
  11.1 1.6 copy-done.2
  12.7 1.2 copy-done.7
  13.9 4.7 %gather_own.1 = (bf16[1024,512]{1,0:T(8,128)(2,1)}, f32[1024,128]{1,0:T(8,128)S(1)}, bf16[4096,128]{1,0:T(8,128)(2,1)S(1)}, bf16[4096,128]{1,0:T(8,128)(2,1)S(1)}, f32[1,4096]{1,0:T(1,128)S(1)}) custom-call(s32[2]{0:T(128)S(1)} %compare_convert_fusion.flags, s32[512,1]{1,0:T(8,128)S(1)} %copy.6.rows_down, s32[1,512]{1,0:T(1,128)S(1)} %broadcast_select_fusion.rows_across, ...), custom_call_target="tpu_custom_call" | custom-call | tf_op jit(solution)/shard_map/gather_own/pallas_call | solution.py:111
  18.7 1.0 copy-done.8
  19.7 1.0 copy-done.10
  21.5 137.7 %all-reduce.3.cloned.1.call-done.arrived = bf16[1024,512]{1,0:T(8,128)(2,1)} async-done(((bf16[1024,512]{1,0:T(8,128)(2,1)}), bf16[1024,512]{1,0:T(8,128)(2,1)}) %all-reduce.3.cloned.1.call-update) | async-done | bytes 1048592 | tf_op jit(solution)/shard_map/psum | solution.py:306
  159.2 2.2 copy-done.1
  161.4 1.2 copy-done.4
  162.7 1.2 copy-done.9
  163.9 1.2 copy-done.11
  165.1 1.0 copy-done.13
  166.2 8.0 %local_terms.1 = f32[1024,128]{1,0:T(8,128)S(1)} custom-call(bf16[1024,512]{1,0:T(8,128)(2,1)S(1)} %copy-done.4, bf16[4096,512]{1,0:T(8,128)(2,1)S(1)} %copy-done.1, f32[1,4096]{1,0:T(1,128)S(1)} %get-tuple-element.15.squares, bf16[4096,128]{1,0:T(8,128)(2,1)S(1)} %copy-done.9, bf16[4096,128]{1,0:T(8,128)(2,1)S(1)} %copy-done.11, f32[1024,128]{1,0:T(8,128)S(1)} %copy-done.13), custom_call_target="tpu_custom_call" | custom-call | tf_op jit(solution)/shard_map/local_terms/pallas_call | solution.py:157
  175.0 12.1 %factor.1 = (f32[2,256,256]{2,1,0:T(8,128)S(1)}, f32[2,256,256]{2,1,0:T(8,128)S(1)}, f32[2,256,256]{2,1,0:T(8,128)S(1)}, bf16[512,512]{1,0:T(8,128)(2,1)S(1)}) custom-call(bf16[1024,512]{1,0:T(8,128)(2,1)S(1)} %copy-done.5), custom_call_target="tpu_custom_call" | custom-call | tf_op jit(solution)/shard_map/factor/pallas_call | solution.py:231
  187.1 0.8 copy-done.15
  187.9 0.8 copy-done.17
  188.7 0.8 copy-done.19
  190.3 111.7 %all-reduce.5.cloned.1.call-done.sides = f32[1024,128]{1,0:T(8,128)} async-done(((f32[1024,128]{1,0:T(8,128)}), f32[1024,128]{1,0:T(8,128)}) %all-reduce.5.cloned.1.call-update) | async-done | bytes 524304 | tf_op jit(solution)/shard_map/psum | solution.py:308
  302.0 1.0 copy-done.14
  303.0 1.0 copy-done.16
  304.1 1.0 copy-done.18
  305.1 1.0 copy-done.20
  306.2 1.0 copy-done.22
  307.2 2.4 finish.1
  (36 shorter events, 4.8 us)
Async XLA Ops:
  6.5 152.7 %all-reduce.3.cloned.1.call-start = ((), (), s32[]{:S(2)}) async-start(), calls=%async_computation | async-start | bytes 2097152 | tf_op jit(solution)/shard_map/psum | solution.py:306
  8.9 2.2 copy-start
  11.1 1.6 copy-start.2
  12.7 1.2 copy-start.7
  18.7 1.0 copy-start.8
  19.6 1.0 copy-start.10
  21.5 280.5 %all-reduce.5.cloned.1.call-start = ((), (), s32[]{:S(2)}) async-start(), calls=%async_computation.1 | async-start | bytes 1048576 | tf_op jit(solution)/shard_map/psum | solution.py:308
  159.2 2.2 copy-start.1
  161.4 1.2 copy-start.4
  162.7 1.2 copy-start.9
  163.9 1.2 copy-start.11
  165.1 1.0 copy-start.13
  166.2 8.9 %copy-start.5 = (bf16[1024,512]{1,0:T(8,128)(2,1)S(1)}, bf16[1024,512]{1,0:T(8,128)(2,1)}, u32[]{:S(2)}) copy-start(bf16[1024,512]{1,0:T(8,128)(2,1)} %all-reduce.3.cloned.1.call-done.arrived) | copy-start | bytes 3145732
  166.2 135.8 %copy-start.3 = (f32[4096,128]{1,0:T(8,128)S(1)}, f32[4096,128]{1,0:T(8,128)}, u32[]{:S(2)}) copy-start(f32[4096,128]{1,0:T(8,128)} %coefs.3) | copy-start | bytes 6291460
  174.2 0.8 copy-start.6
  187.1 0.8 copy-start.15
  187.9 0.8 copy-start.17
  188.7 0.8 copy-start.19
  189.5 0.8 copy-start.21
  302.0 1.0 copy-start.14
  303.0 1.0 copy-start.16
  304.1 1.0 copy-start.18
  305.1 1.0 copy-start.20
  306.2 1.0 copy-start.22
  (1 other events, 0.8 us)
Sparse Core Ops, SparseCore 0:
  21.6 137.6 all-reduce.2
  175.1 126.8 all-reduce.4

commit v2 on v1

--- a/solution.py
+++ b/solution.py
@@ -49,6 +49,107 @@
     high, low = halves(widened * widened)
     ones = jnp.ones((8, rows.shape[1]), bf16)
     return (nt_dot(ones, high) + nt_dot(ones, low))[0:1]
+
+
+def cube_orders(wide, narrow):
+    bits = [("narrow", 1 << k) for k in range(narrow.bit_length() - 1)]
+    bits += [("wide", 1 << k) for k in range(wide.bit_length() - 1)]
+    turned = bits[:1] + bits[2:-1] + bits[1:2] + bits[-1:]
+    return bits, turned if len(bits) > 3 else bits
+
+
+def cube_kernel(orders, value, out, *scratch):
+    steps = len(orders[0])
+    kept, sems = scratch[:-1], scratch[-1]
+    chunks = 1 << steps
+
+    def side(bit):
+        axis, weight = bit
+        return lax.rem(lax.axis_index(axis) // weight, 2)
+
+    def partner(bit):
+        axis, weight = bit
+        place = {name: lax.axis_index(name) for name in ("wide", "narrow")}
+        place[axis] = place[axis] + weight - 2 * weight * side(bit)
+        return (place["wide"], place["narrow"])
+
+    def copy(source, target, bit, part, step, phase):
+        return pltpu.make_async_remote_copy(
+            src_ref=source, dst_ref=target, send_sem=sems.at[0, phase, part, step], recv_sem=sems.at[1, phase, part, step],
+            device_id=partner(bit), device_id_type=pl.DeviceIdType.MESH,
+        )
+
+    barrier = pltpu.get_barrier_semaphore()
+    for bit in orders[0]:
+        pl.semaphore_signal(barrier, inc=1, device_id=partner(bit), device_id_type=pl.DeviceIdType.MESH)
+    pl.semaphore_wait(barrier, steps)
+
+    def held(part, step):
+        if step < 0:
+            return value.at[pl.ds(part * chunks, chunks)]
+        return kept[part * steps + step]
+
+    started = []
+    flying = {}
+
+    def absorb(part, step):
+        count = chunks >> (step + 1)
+        flying[part].wait_recv()
+        spot = held(part, step)
+        spot[...] = spot[...] + held(part, step - 1)[pl.ds(side(orders[part][step]) * count, count)]
+
+    for step in range(steps):
+        count = chunks >> (step + 1)
+        for part, order in enumerate(orders):
+            if step > 0:
+                absorb(part, step - 1)
+            away = (1 - side(order[step])) * count
+            flying[part] = copy(held(part, step - 1).at[pl.ds(away, count)], held(part, step), order[step], part, step, 0)
+            flying[part].start()
+            started.append(flying[part])
+    bases = []
+    for part, order in enumerate(orders):
+        absorb(part, steps - 1)
+        base = part * chunks
+        listed = []
+        for step in range(steps):
+            base = base + side(order[step]) * (chunks >> (step + 1))
+            listed.append(base)
+        bases.append(listed)
+        out[pl.ds(base, 1)] = held(part, steps - 1)[...]
+    for step in reversed(range(steps)):
+        count = chunks >> (step + 1)
+        for part, order in enumerate(orders):
+            if step < steps - 1:
+                flying[part].wait_recv()
+            span = out.at[pl.ds(bases[part][step], count)]
+            flying[part] = copy(span, span, order[step], part, step, 1)
+            flying[part].start()
+            started.append(flying[part])
+    for part in range(len(orders)):
+        flying[part].wait_recv()
+    for sent in started:
+        sent.wait_send()
+
+
+def cube_sum(value, wide, narrow, number):
+    orders = cube_orders(wide, narrow)
+    steps = len(orders[0])
+    chunks = 1 << steps
+    rows, columns = value.shape
+    depth = rows // (2 * chunks)
+    shape = (2 * chunks, depth, columns)
+    slots = [pltpu.VMEM((chunks >> (step + 1), depth, columns), value.dtype) for _ in orders for step in range(steps)]
+    summed = pl.pallas_call(
+        functools.partial(cube_kernel, orders),
+        in_specs=[whole_vmem],
+        out_specs=whole_vmem,
+        out_shape=jax.ShapeDtypeStruct(shape, value.dtype),
+        scratch_shapes=slots + [pltpu.SemaphoreType.DMA((2, 2, 2, steps))],
+        compiler_params=pltpu.CompilerParams(collective_id=number, has_side_effects=True, vmem_limit_bytes=40 << 20),
+        name="cube_sum",
+    )(value.reshape(shape))
+    return summed.reshape(rows, columns)
 
 
 def gather_kernel(flags, rows_down, rows_across, feats, coefs, targs, spread_out, targ_out, mask0_out, mask1_out,
@@ -303,9 +404,10 @@
     flags = (block_owner == device).astype(jnp.int32)
     rows = jnp.where(flags[0] > 0, block_rows[0], block_rows[1])
     spread, own, mask0, mask1, squares = gather_own(flags, rows, features, coefficients, targets)
-    arrived = lax.psum(spread, ("wide", "narrow"))
+    sizes = lax.axis_size("wide"), lax.axis_size("narrow")
+    arrived = cube_sum(spread, *sizes, 0)
     terms = local_terms(arrived, features, squares, mask0, mask1, own)
-    sides = lax.psum(terms, ("wide", "narrow"))
+    sides = cube_sum(terms, *sizes, 1)
     parts = factor(arrived)
     return finish(flags, rows, coefficients, sides, *parts)
 

time: 320 us -> 105 us (0.33)
  waiting for transfers between devices: 249 us -> 0 us
  Pallas kernels: 27.2 us -> 95.7 us
  local copies, waits for them, and re-layouts: 24 us -> 5.16 us
  between operations: 13.5 us -> 0.13 us
    psum x2 -> x0, waiting for transfers between devices: 249 us -> none  [the longest x1 138 us: per_device(): arrived = lax.psum(spread, ('wide', 'narrow'))]
    pallas_call x0 -> x2, Pallas kernels: none -> 69.4 us  [cube_sum(): pl.pallas_call(functools.partial(cube_kernel, orders), in_specs=[whole_vm...]
    unnamed x46 -> x10, local copies, waits for them, and re-layouts: 23.8 us -> 5.01 us
  transfers between devices with their start and end apart: 2 -> 0, of which waited for: 2 -> 0; matrix products, arithmetic and copies ran while one was open for 0% -> 0% of each run, Pallas kernels for 4% -> 0%
where the time goes in v2:
time: 105 us; the launch traced here: 103 us
  Pallas kernels  95.7 us (91%)
  local copies, waits for them, and re-layouts  5.16 us (5%)
  other arithmetic  2.19 us (2%)
    pallas_call x2, Pallas kernels, cube_sum(): pl.pallas_call(functools.partial(cube_kernel, orders), in_specs=[whole_vm...  69.4 us
    pallas_call x1, Pallas kernels, factor(): pl.pallas_call(factor_kernel, in_specs=[whole_vmem], out_specs=[whole_vme...  12.1 us
    pallas_call x1, Pallas kernels, local_terms(): pl.pallas_call(terms_kernel, grid=(count // tile,), in_specs=[still(arriv...  8.07 us
    unnamed x10, local copies, waits for them, and re-layouts  5.01 us
    pallas_call x1, Pallas kernels, gather_own(): pl.pallas_call(gather_kernel, grid=(count // tile,), in_specs=[whole_smem...  3.77 us
    pallas_call x1, Pallas kernels, finish(): pl.pallas_call(finish_kernel, grid=(count // tile,), in_specs=[whole_smem...  2.43 us

profile of v2, /device:TPU:0, one launch (start us, length us, event | category | flops | bytes accessed | tf_op | source)
XLA Modules:
  0.0 103.2 jit_solution(13969498180611731145)
XLA Ops:
  0.0 0.7 compare_convert_fusion.flags
  0.7 0.8 broadcast_select_fusion.rows_across
  1.5 0.8 fusion
  2.2 0.1 copy.6.rows_down
  2.4 0.0 copy-start
  2.4 2.2 %copy-done = bf16[4096,512]{1,0:T(8,128)(2,1)S(1)} copy-done((bf16[4096,512]{1,0:T(8,128)(2,1)S(1)}, bf16[4096,512]{1,0:T(8,128)(2,1)}, u32[]{:S(2)}) %copy-start) | copy-done | bytes 4194328
  4.6 0.0 copy-start.2
  4.6 1.6 %copy-done.2 = f32[4096,128]{1,0:T(8,128)S(1)} copy-done((f32[4096,128]{1,0:T(8,128)S(1)}, f32[4096,128]{1,0:T(8,128)}, u32[]{:S(2)}) %copy-start.2) | copy-done | bytes 2097176
  6.2 0.0 copy-start.4
  6.2 1.2 %copy-done.4 = bf16[4096,128]{1,0:T(8,128)(2,1)S(1)} copy-done((bf16[4096,128]{1,0:T(8,128)(2,1)S(1)}, bf16[4096,128]{1,0:T(8,128)(2,1)}, u32[]{:S(2)}) %copy-start.4) | copy-done | bytes 1048600
  7.4 0.0 copy-start.1
  7.4 3.8 %gather_own.1 = (bf16[1024,512]{1,0:T(8,128)(2,1)S(1)}, f32[1024,128]{1,0:T(8,128)S(1)}, bf16[4096,128]{1,0:T(8,128)(2,1)S(1)}, bf16[4096,128]{1,0:T(8,128)(2,1)S(1)}, f32[1,4096]{1,0:T(1,128)S(1)}) custom-call(s32[2]{0:T(128)S(1)} %compare_convert_fusion.flags, s32[512,1]{1,0:T(8,128)S(1)} %copy.6.rows_down, s32[1,512]{1,0:T(1,128)S(1)} %broadcast_select_fusion.rows_across, ...), custom_call_target="tpu_custom_call" | custom-call | tf_op jit(solution)/shard_map/gather_own/pallas_call | solution.py:212
  11.2 39.4 %cube_sum.2 = bf16[64,16,512]{2,1,0:T(8,128)(2,1)S(1)} custom-call(bf16[64,16,512]{2,1,0:T(8,128)(2,1)S(1)} %bitcast.12), custom_call_target="tpu_custom_call" | custom-call | tf_op jit(solution)/shard_map/cube_sum/pallas_call | solution.py:143
  50.6 0.0 copy-done.1
  50.6 8.1 %local_terms.1 = f32[1024,128]{1,0:T(8,128)S(1)} custom-call(bf16[1024,512]{1,0:T(8,128)(2,1)S(1)} %bitcast.8, bf16[4096,512]{1,0:T(8,128)(2,1)S(1)} %copy-done.1, f32[1,4096]{1,0:T(1,128)S(1)} %get-tuple-element.15.squares, bf16[4096,128]{1,0:T(8,128)(2,1)S(1)} %get-tuple-element.16.mask0, bf16[4096,128]{1,0:T(8,128)(2,1)S(1)} %get-tuple-element.17.mask1, ...), custom_call_target="tpu_custom_call" | custom-call | tf_op jit(solution)/shard_map/local_terms/pallas_call | solution.py:258
  58.6 0.0 copy-start.3
  58.7 30.1 %cube_sum.3 = f32[64,16,128]{2,1,0:T(8,128)S(1)} custom-call(f32[64,16,128]{2,1,0:T(8,128)S(1)} %bitcast.11), custom_call_target="tpu_custom_call" | custom-call | tf_op jit(solution)/shard_map/cube_sum/pallas_call | solution.py:143
  88.7 12.1 %factor.1 = (f32[2,256,256]{2,1,0:T(8,128)S(1)}, f32[2,256,256]{2,1,0:T(8,128)S(1)}, f32[2,256,256]{2,1,0:T(8,128)S(1)}, bf16[512,512]{1,0:T(8,128)(2,1)S(1)}) custom-call(bf16[1024,512]{1,0:T(8,128)(2,1)S(1)} %bitcast.9), custom_call_target="tpu_custom_call" | custom-call | tf_op jit(solution)/shard_map/factor/pallas_call | solution.py:332
  100.8 0.0 copy-done.3
  100.8 2.4 %finish.1 = f32[4096,128]{1,0:T(8,128)} custom-call(s32[2]{0:T(128)S(1)} %compare_convert_fusion.flags, s32[1,512]{1,0:T(1,128)S(1)} %broadcast_select_fusion.rows_across, f32[4096,128]{1,0:T(8,128)S(1)} %copy-done.3, f32[1024,128]{1,0:T(8,128)S(1)} %bitcast.10, f32[2,256,256]{2,1,0:T(8,128)S(1)} %get-tuple-element.19.first_inv, ...), custom_call_target="tpu_custom_call" | custom-call | tf_op jit(solution)/shard_map/finish/pallas_call | solution.py:390
Async XLA Ops:
  2.4 2.2 %copy-start = (bf16[4096,512]{1,0:T(8,128)(2,1)S(1)}, bf16[4096,512]{1,0:T(8,128)(2,1)}, u32[]{:S(2)}) copy-start(bf16[4096,512]{1,0:T(8,128)(2,1)} %feats.3) | copy-start | bytes 12582916
  4.6 1.6 %copy-start.2 = (f32[4096,128]{1,0:T(8,128)S(1)}, f32[4096,128]{1,0:T(8,128)}, u32[]{:S(2)}) copy-start(f32[4096,128]{1,0:T(8,128)} %coefs.3) | copy-start | bytes 6291460
  6.2 1.2 %copy-start.4 = (bf16[4096,128]{1,0:T(8,128)(2,1)S(1)}, bf16[4096,128]{1,0:T(8,128)(2,1)}, u32[]{:S(2)}) copy-start(bf16[4096,128]{1,0:T(8,128)(2,1)} %targs.1) | copy-start | bytes 3145732
  7.4 43.1 %copy-start.1 = (bf16[4096,512]{1,0:T(8,128)(2,1)S(1)}, bf16[4096,512]{1,0:T(8,128)(2,1)}, u32[]{:S(2)}) copy-start(bf16[4096,512]{1,0:T(8,128)(2,1)} %feats.3) | copy-start | bytes 12582916
  58.6 42.1 %copy-start.3 = (f32[4096,128]{1,0:T(8,128)S(1)}, f32[4096,128]{1,0:T(8,128)}, u32[]{:S(2)}) copy-start(f32[4096,128]{1,0:T(8,128)} %coefs.3) | copy-start | bytes 6291460

commit v3 on v2

--- a/solution.py
+++ b/solution.py
@@ -51,15 +51,24 @@
     return (nt_dot(ones, high) + nt_dot(ones, low))[0:1]
 
 
-def cube_orders(wide, narrow):
+def cube_orders(wide, narrow, parts):
     bits = [("narrow", 1 << k) for k in range(narrow.bit_length() - 1)]
     bits += [("wide", 1 << k) for k in range(wide.bit_length() - 1)]
-    turned = bits[:1] + bits[2:-1] + bits[1:2] + bits[-1:]
-    return bits, turned if len(bits) > 3 else bits
-
-
-def cube_kernel(orders, value, out, *scratch):
+    inner = bits[1:-1]
+    turned = [bits[:1] + inner[turn:] + inner[:turn] + bits[-1:] for turn in range(max(len(inner), 1))]
+    return [turned[part % len(turned)] for part in range(parts)]
+
+
+def cube_kernel(orders, extra, value, *refs):
     steps = len(orders[0])
+    if extra:
+        arrived, out, *results = refs[:6]
+        scratch = refs[6:]
+        work = factor_pieces(arrived, *results)
+    else:
+        out, *scratch = refs
+        work = iter(())
+    share = 2
     kept, sems = scratch[:-1], scratch[-1]
     chunks = 1 << steps
 
@@ -107,6 +116,8 @@
             flying[part] = copy(held(part, step - 1).at[pl.ds(away, count)], held(part, step), order[step], part, step, 0)
             flying[part].start()
             started.append(flying[part])
+        for _ in range(share):
+            next(work, None)
     bases = []
     for part, order in enumerate(orders):
         absorb(part, steps - 1)
@@ -126,38 +137,61 @@
             flying[part] = copy(span, span, order[step], part, step, 1)
             flying[part].start()
             started.append(flying[part])
+        for _ in range(share):
+            next(work, None)
+    for _ in work:
+        pass
     for part in range(len(orders)):
         flying[part].wait_recv()
     for sent in started:
         sent.wait_send()
 
 
-def cube_sum(value, wide, narrow, number):
-    orders = cube_orders(wide, narrow)
+def cube_sum(value, wide, narrow, number, arrived=None):
+    rows, columns = value.shape
+    chunks = wide * narrow
+    parts = 4 if rows // (4 * chunks) >= 8 else 2
+    orders = cube_orders(wide, narrow, parts)
     steps = len(orders[0])
-    chunks = 1 << steps
-    rows, columns = value.shape
-    depth = rows // (2 * chunks)
-    shape = (2 * chunks, depth, columns)
+    depth = rows // (parts * chunks)
+    shape = (parts * chunks, depth, columns)
     slots = [pltpu.VMEM((chunks >> (step + 1), depth, columns), value.dtype) for _ in orders for step in range(steps)]
-    summed = pl.pallas_call(
-        functools.partial(cube_kernel, orders),
-        in_specs=[whole_vmem],
-        out_specs=whole_vmem,
-        out_shape=jax.ShapeDtypeStruct(shape, value.dtype),
-        scratch_shapes=slots + [pltpu.SemaphoreType.DMA((2, 2, 2, steps))],
+    extra = () if arrived is None else (arrived,)
+    shapes = [jax.ShapeDtypeStruct(shape, value.dtype)]
+    if extra:
+        block = arrived.shape[0] // 2
+        square = jax.ShapeDtypeStruct((2, block // 2, block // 2), f32)
+        shapes += [square, square, square, jax.ShapeDtypeStruct((block, block), bf16)]
+    summed, *results = pl.pallas_call(
+        functools.partial(cube_kernel, orders, bool(extra)),
+        in_specs=[whole_vmem] * (1 + len(extra)),
+        out_specs=[whole_vmem] * len(shapes),
+        out_shape=shapes,
+        scratch_shapes=slots + [pltpu.SemaphoreType.DMA((2, 2, parts, steps))],
         compiler_params=pltpu.CompilerParams(collective_id=number, has_side_effects=True, vmem_limit_bytes=40 << 20),
         name="cube_sum",
-    )(value.reshape(shape))
-    return summed.reshape(rows, columns)
-
-
-def gather_kernel(flags, rows_down, rows_across, feats, coefs, targs, spread_out, targ_out, mask0_out, mask1_out,
+    )(value.reshape(shape), *extra)
+    return summed.reshape(rows, columns), results
+
+
+def own_flags(owners):
+    device = lax.axis_index("wide") * lax.axis_size("narrow") + lax.axis_index("narrow")
+    return [jnp.where(owners[index] == device, 1, 0) for index in range(2)]
+
+
+def place_rows(first, listed, tile, step):
+    block = listed.shape[1]
+    rows = jnp.where(first > 0, listed[0:1, :], listed[1:2, :])
+    subs = lax.broadcasted_iota(jnp.int32, (tile, block), 0) + step * tile
+    return jnp.where(subs == rows, 1.0, 0.0).astype(bf16)
+
+
+def gather_kernel(owners, listed, feats, coefs, targs, spread_out, targ_out, mask0_out, mask1_out,
                   squares_out, feat_total, targ_total):
     step = pl.program_id(0)
     tile = feats.shape[0]
-    block = rows_down.shape[0]
-    first, second = flags[0], flags[1]
+    block = listed.shape[1]
+    first, second = own_flags(owners)
     squares_out[...] = lane_squares(feats[...])
     plain = coefs[...].astype(bf16)
 
@@ -173,12 +207,9 @@
 
     @pl.when(first + second > 0)
     def _():
-        lanes = lax.broadcasted_iota(jnp.int32, (block, tile), 1) + step * tile
-        pick = jnp.where(lanes == rows_down[...], 1.0, 0.0).astype(bf16)
-        feat_part = nn_dot(pick, feats[...])
-        targ_part = nn_dot(pick, targs[...])
-        subs = lax.broadcasted_iota(jnp.int32, (tile, block), 0) + step * tile
-        place = jnp.where(subs == rows_across[...], 1.0, 0.0).astype(bf16)
+        place = place_rows(first, listed, tile, step)
+        feat_part = tn_dot(place, feats[...])
+        targ_part = tn_dot(place, targs[...])
         taken = nn_dot(place, jnp.ones((block, coefs.shape[1]), bf16)) > 0.5
         cleared = jnp.where(taken, 0.0, coefs[...]).astype(bf16)
         mask0_out[...] = jnp.where(first > 0, cleared, plain)
@@ -202,17 +233,17 @@
                 targ_out[pl.ds(index * block, block), :] = jnp.where(keep, targ_total[...], 0.0)
 
 
-def gather_own(flags, rows, features, coefficients, targets):
+def gather_own(owners, listed, features, coefficients, targets):
     count, width = features.shape
     outs = coefficients.shape[1]
-    block = rows.shape[0]
+    block = listed.shape[1]
     tile = min(1024, count)
     moving = lambda columns: pl.BlockSpec((tile, columns), lambda i: (i, 0))
     still = lambda shape: pl.BlockSpec(shape, lambda i: (0, 0))
     return pl.pallas_call(
         gather_kernel,
         grid=(count // tile,),
-        in_specs=[whole_smem, still((block, 1)), still((1, block)), moving(width), moving(outs), moving(outs)],
+        in_specs=[whole_smem, still(listed.shape), moving(width), moving(outs), moving(outs)],
         out_specs=[
             still((2 * block, width)), still((2 * block, outs)), moving(outs), moving(outs),
             pl.BlockSpec((1, tile), lambda i: (0, i)),
@@ -223,9 +254,9 @@
             jax.ShapeDtypeStruct((1, count), f32),
         ],
         scratch_shapes=[pltpu.VMEM((block, width), f32), pltpu.VMEM((block, outs), f32)],
-        compiler_params=pltpu.CompilerParams(vmem_limit_bytes=40 << 20),
+        compiler_params=pltpu.CompilerParams(vmem_limit_bytes=58 << 20),
         name="gather_own",
-    )(flags, rows[:, None], rows[None, :], features, coefficients, targets)
+    )(owners, listed, features, coefficients, targets)
 
 
 def terms_kernel(arrived, feats, squares, mask0, mask1, own, terms_out, offsets):
@@ -289,15 +320,17 @@
     )
     for index, matrix in enumerate(matrices):
         keep[index] = (2.0 * start * scales[0]) * eye - (start * start * scales[0]) * matrix
+    yield
     for scale in scales[1:]:
         guesses = [keep[index] for index in range(2)]
         rests = [fine_dot(matrix, guess) for matrix, guess in zip(matrices, guesses)]
         for index in range(2):
             change = fine_dot(guesses[index], rests[index])
             keep[index] = (2.0 * scale) * guesses[index] - scale * change
-
-
-def factor_kernel(arrived, first_out, cross_out, second_out, between_out):
+        yield
+
+
+def factor_pieces(arrived, first_out, cross_out, second_out, between_out):
     width = arrived.shape[1]
     block = arrived.shape[0] // 2
     half = block // 2
@@ -313,35 +346,22 @@
         lax.broadcasted_iota(jnp.int32, (half, half), 0) == lax.broadcasted_iota(jnp.int32, (half, half), 1),
         ridge_term, 0.0,
     )
-    invert_pair([values(span(i, 0), span(i, 0)) + ridge for i in range(2)], first_out)
+    yield from invert_pair([values(span(i, 0), span(i, 0)) + ridge for i in range(2)], first_out)
     rests = []
     for i in range(2):
         low = values(span(i, 1), span(i, 0))
         cross = fine_dot(low, first_out[i])
         cross_out[i] = cross
         rests.append(values(span(i, 1), span(i, 1)) + ridge - fine_dot(cross, low, nt_dot))
-    invert_pair(rests, second_out)
+    yield from invert_pair(rests, second_out)
     for part in range(2):
         between_out[pl.ds(part * half, half), :] = values(span(1, part), pl.ds(0, block)).astype(bf16)
 
 
-def factor(arrived):
-    block = arrived.shape[0] // 2
-    half = block // 2
-    shape = jax.ShapeDtypeStruct((2, half, half), f32)
-    return pl.pallas_call(
-        factor_kernel,
-        in_specs=[whole_vmem],
-        out_specs=[whole_vmem] * 4,
-        out_shape=[shape, shape, shape, jax.ShapeDtypeStruct((block, block), bf16)],
-        compiler_params=pltpu.CompilerParams(vmem_limit_bytes=40 << 20),
-        name="factor",
-    )(arrived)
-
-
-def finish_kernel(flags, rows_across, coefs, sides, first_inv, cross, second_inv, between, out, pieces):
+def finish_kernel(owners, listed, coefs, sides, first_inv, cross, second_inv, between, out, pieces):
     step = pl.program_id(0)
-    block = rows_across.shape[1]
+    block = listed.shape[1]
+    first, second = own_flags(owners)
     half = block // 2
     tile, outs = coefs.shape
 
@@ -351,7 +371,7 @@
         high_part = fine_dot(first_inv[index], upper) - fine_dot(cross[index], low_part, tn_dot)
         return high_part, low_part
 
-    mine = flags[0] + flags[1] > 0
+    mine = first + second > 0
 
     @pl.when(mine & (step == 0))
     def _():
@@ -360,7 +380,7 @@
         moved = nn_dot(between[...], sent)
         later = solve(1, sides[pl.ds(block, half), :] - moved[:half], sides[pl.ds(block + half, half), :] - moved[half:])
         for part in range(2):
-            value = jnp.where(flags[0] > 0, fresh[part], later[part])
+            value = jnp.where(first > 0, fresh[part], later[part])
             high = value.astype(bf16)
             rest = value - high.astype(f32)
             mid = rest.astype(bf16)
@@ -371,8 +391,7 @@
 
     @pl.when(mine)
     def _():
-        subs = lax.broadcasted_iota(jnp.int32, (tile, block), 0) + step * tile
-        place = jnp.where(subs == rows_across[...], 1.0, 0.0).astype(bf16)
+        place = place_rows(first, listed, tile, step)
         spread = nn_dot(place, pieces[...])
         value = spread[:, :outs] + spread[:, outs : 2 * outs] + spread[:, 2 * outs : 3 * outs]
         out[...] = jnp.where(spread[:, 3 * outs :] > 0.5, value, coefs[...])
@@ -382,9 +401,9 @@
         out[...] = coefs[...]
 
 
-def finish(flags, rows, coefficients, sides, first_inv, cross, second_inv, between):
+def finish(owners, listed, coefficients, sides, first_inv, cross, second_inv, between):
     count, outs = coefficients.shape
-    block = rows.shape[0]
+    block = listed.shape[1]
     tile = min(1024, count)
     moving = pl.BlockSpec((tile, outs), lambda i: (i, 0))
     return pl.pallas_call(
@@ -396,20 +415,16 @@
         scratch_shapes=[pltpu.VMEM((block, 4 * outs), bf16)],
         compiler_params=pltpu.CompilerParams(vmem_limit_bytes=40 << 20),
         name="finish",
-    )(flags, rows[None, :], coefficients, sides, first_inv, cross, second_inv, between)
+    )(owners, listed, coefficients, sides, first_inv, cross, second_inv, between)
 
 
 def per_device(features, coefficients, targets, block_rows, block_owner):
-    device = lax.axis_index("wide") * lax.axis_size("narrow") + lax.axis_index("narrow")
-    flags = (block_owner == device).astype(jnp.int32)
-    rows = jnp.where(flags[0] > 0, block_rows[0], block_rows[1])
-    spread, own, mask0, mask1, squares = gather_own(flags, rows, features, coefficients, targets)
     sizes = lax.axis_size("wide"), lax.axis_size("narrow")
-    arrived = cube_sum(spread, *sizes, 0)
+    spread, own, mask0, mask1, squares = gather_own(block_owner, block_rows, features, coefficients, targets)
+    arrived, _ = cube_sum(spread, *sizes, 0)
     terms = local_terms(arrived, features, squares, mask0, mask1, own)
-    sides = cube_sum(terms, *sizes, 1)
-    parts = factor(arrived)
-    return finish(flags, rows, coefficients, sides, *parts)
+    sides, parts = cube_sum(terms, *sizes, 1, arrived)
+    return finish(block_owner, block_rows, coefficients, sides, *parts)
 
 
 def solution(mesh):

time: 105 us -> 88.2 us (0.84)
  Pallas kernels: 95.7 us -> 83.5 us
  other arithmetic: 2.19 us -> 0 us
  local copies, waits for them, and re-layouts: 5.16 us -> 2.99 us
    pallas_call x3 -> x2, Pallas kernels: 81.5 us -> 65.6 us  [cube_sum(): pl.pallas_call(functools.partial(cube_kernel, orders, bool(extra)), in_sp...]
    pallas_call x1, Pallas kernels: 3.77 us -> 7.35 us  [gather_own(): pl.pallas_call(gather_kernel, grid=(count // tile,), in_specs=[whole_smem...]
    unnamed x10 -> x18, local copies, waits for them, and re-layouts: 5.01 us -> 2.99 us
    select_n x2 -> x0, other arithmetic: 1.54 us -> none  [per_device(): rows = jnp.where(flags[0] > 0, block_rows[0], block_rows[1])]
where the time goes in v3:
time: 88.2 us; the launch traced here: 86.5 us
  Pallas kernels  83.5 us (95%)
  local copies, waits for them, and re-layouts  2.99 us (3%)
    pallas_call x2, Pallas kernels, cube_sum(): pl.pallas_call(functools.partial(cube_kernel, orders, bool(extra)), in_sp...  65.6 us
    pallas_call x1, Pallas kernels, local_terms(): pl.pallas_call(terms_kernel, grid=(count // tile,), in_specs=[still(arriv...  8.01 us
    pallas_call x1, Pallas kernels, gather_own(): pl.pallas_call(gather_kernel, grid=(count // tile,), in_specs=[whole_smem...  7.35 us
    unnamed x18, local copies, waits for them, and re-layouts  2.99 us
    pallas_call x1, Pallas kernels, finish(): pl.pallas_call(finish_kernel, grid=(count // tile,), in_specs=[whole_smem...  2.46 us

profile of v3, /device:TPU:0, one launch (start us, length us, event | category | flops | bytes accessed | tf_op | source)
XLA Modules:
  0.0 86.5 jit_solution(8057833398690495158)
XLA Ops:
  0.0 0.0 copy-start
  0.0 7.3 %gather_own.1 = (bf16[1024,512]{1,0:T(8,128)(2,1)}, f32[1024,128]{1,0:T(8,128)}, bf16[4096,128]{1,0:T(8,128)(2,1)}, bf16[4096,128]{1,0:T(8,128)(2,1)}, f32[1,4096]{1,0:T(1,128)}) custom-call(s32[2]{0:T(128)} %owners.3, s32[2,512]{1,0:T(2,128)} %listed.3, bf16[4096,512]{1,0:T(8,128)(2,1)} %feats.3, f32[4096,128]{1,0:T(8,128)} %coefs.3, bf16[4096,128]{1,0:T(8,128)(2,1)} %targs.1), custom_call_target="tpu_custom_call" | custom-call | tf_op jit(solution)/shard_map/gather_own/pallas_call | solution.py:243
  7.3 0.0 copy-start.2
  7.4 1.2 %copy-done.2 = bf16[1024,512]{1,0:T(8,128)(2,1)S(1)} copy-done((bf16[1024,512]{1,0:T(8,128)(2,1)S(1)}, bf16[1024,512]{1,0:T(8,128)(2,1)}, u32[]{:S(2)}) %copy-start.2) | copy-done | bytes 1048600
  8.6 0.0 copy-start.3
  8.6 0.0 copy-start.4
  8.6 37.9 %cube_sum.2 = bf16[128,8,512]{2,1,0:T(8,128)(2,1)S(1)} custom-call(bf16[128,8,512]{2,1,0:T(8,128)(2,1)S(1)} %bitcast.7), custom_call_target="tpu_custom_call" | custom-call | tf_op jit(solution)/shard_map/cube_sum/pallas_call | solution.py:165
  46.5 0.0 copy-done
  46.5 0.0 copy-done.3
  46.5 0.0 copy-done.4
  46.5 0.0 copy-start.5
  46.5 1.0 %copy-done.5 = f32[1024,128]{1,0:T(8,128)S(1)} copy-done((f32[1024,128]{1,0:T(8,128)S(1)}, f32[1024,128]{1,0:T(8,128)}, u32[]{:S(2)}) %copy-start.5) | copy-done | bytes 524312
  47.6 0.0 copy-start.7
  47.6 0.7 copy-done.7
  48.3 0.0 copy-start.1
  48.3 0.0 copy-start.6
  48.3 0.0 copy-start.8
  48.3 8.0 %local_terms.1 = f32[1024,128]{1,0:T(8,128)S(1)} custom-call(bf16[1024,512]{1,0:T(8,128)(2,1)S(1)} %bitcast.4, bf16[4096,512]{1,0:T(8,128)(2,1)S(1)} %copy-done, f32[1,4096]{1,0:T(1,128)S(1)} %copy-done.7, bf16[4096,128]{1,0:T(8,128)(2,1)S(1)} %copy-done.3, bf16[4096,128]{1,0:T(8,128)(2,1)S(1)} %copy-done.4, f32[1024,128]{1,0:T(8,128)S(1)} %copy-done.5), custom_call_target="tpu_custom_call" | custom-call | tf_op jit(solution)/shard_map/local_terms/pallas_call | solution.py:289
  56.3 27.7 %cube_sum.3 = (f32[128,8,128]{2,1,0:T(8,128)S(1)}, f32[2,256,256]{2,1,0:T(8,128)S(1)}, f32[2,256,256]{2,1,0:T(8,128)S(1)}, f32[2,256,256]{2,1,0:T(8,128)S(1)}, bf16[512,512]{1,0:T(8,128)(2,1)S(1)}) custom-call(f32[128,8,128]{2,1,0:T(8,128)S(1)} %bitcast.6, bf16[1024,512]{1,0:T(8,128)(2,1)S(1)} %bitcast.5), custom_call_target="tpu_custom_call" | custom-call | tf_op jit(solution)/shard_map/cube_sum/pallas_call | solution.py:165
  84.1 0.0 copy-done.1
  84.1 0.0 copy-done.6
  84.1 0.0 copy-done.8
  84.1 2.5 %finish.1 = f32[4096,128]{1,0:T(8,128)} custom-call(s32[2]{0:T(128)S(1)} %copy-done.8, s32[2,512]{1,0:T(2,128)S(1)} %copy-done.6, f32[4096,128]{1,0:T(8,128)S(1)} %copy-done.1, f32[1024,128]{1,0:T(8,128)S(1)} %bitcast.8, f32[2,256,256]{2,1,0:T(8,128)S(1)} %get-tuple-element.21.first_inv, f32[2,256,256]{2,1,0:T(8,128)S(1)} %get-tuple-element.22.cross, ...), custom_call_target="tpu_custom_call" | custom-call | tf_op jit(solution)/shard_map/finish/pallas_call | solution.py:409
Async XLA Ops:
  0.0 46.5 %copy-start = (bf16[4096,512]{1,0:T(8,128)(2,1)S(1)}, bf16[4096,512]{1,0:T(8,128)(2,1)}, u32[]{:S(2)}) copy-start(bf16[4096,512]{1,0:T(8,128)(2,1)} %feats.3) | copy-start | bytes 12582916
  7.3 1.2 %copy-start.2 = (bf16[1024,512]{1,0:T(8,128)(2,1)S(1)}, bf16[1024,512]{1,0:T(8,128)(2,1)}, u32[]{:S(2)}) copy-start(bf16[1024,512]{1,0:T(8,128)(2,1)} %get-tuple-element.15) | copy-start | bytes 3145732
  8.6 37.9 %copy-start.3 = (bf16[4096,128]{1,0:T(8,128)(2,1)S(1)}, bf16[4096,128]{1,0:T(8,128)(2,1)}, u32[]{:S(2)}) copy-start(bf16[4096,128]{1,0:T(8,128)(2,1)} %get-tuple-element.17.mask0) | copy-start | bytes 3145732
  8.6 38.0 %copy-start.4 = (bf16[4096,128]{1,0:T(8,128)(2,1)S(1)}, bf16[4096,128]{1,0:T(8,128)(2,1)}, u32[]{:S(2)}) copy-start(bf16[4096,128]{1,0:T(8,128)(2,1)} %get-tuple-element.18.mask1) | copy-start | bytes 3145732
  46.5 1.0 %copy-start.5 = (f32[1024,128]{1,0:T(8,128)S(1)}, f32[1024,128]{1,0:T(8,128)}, u32[]{:S(2)}) copy-start(f32[1024,128]{1,0:T(8,128)} %get-tuple-element.19.own) | copy-start | bytes 1572868
  47.6 0.7 copy-start.7
  48.3 35.8 %copy-start.1 = (f32[4096,128]{1,0:T(8,128)S(1)}, f32[4096,128]{1,0:T(8,128)}, u32[]{:S(2)}) copy-start(f32[4096,128]{1,0:T(8,128)} %coefs.3) | copy-start | bytes 6291460
  48.3 35.8 %copy-start.6 = (s32[2,512]{1,0:T(2,128)S(1)}, s32[2,512]{1,0:T(2,128)}, u32[]{:S(2)}) copy-start(s32[2,512]{1,0:T(2,128)} %listed.3) | copy-start | bytes 12292
  48.3 35.8 %copy-start.8 = (s32[2]{0:T(128)S(1)}, s32[2]{0:T(128)}, u32[]{:S(2)}) copy-start(s32[2]{0:T(128)} %owners.3) | copy-start | bytes 28

commit v4 on v3

--- a/solution.py
+++ b/solution.py
@@ -54,12 +54,20 @@
 def cube_orders(wide, narrow, parts):
     bits = [("narrow", 1 << k) for k in range(narrow.bit_length() - 1)]
     bits += [("wide", 1 << k) for k in range(wide.bit_length() - 1)]
-    inner = bits[1:-1]
-    turned = [bits[:1] + inner[turn:] + inner[:turn] + bits[-1:] for turn in range(max(len(inner), 1))]
-    return [turned[part % len(turned)] for part in range(parts)]
-
-
-def cube_kernel(orders, extra, value, *refs):
+    groups = [bits[:1]] + [bits[at : at + 2] for at in range(1, len(bits), 2)]
+    inner = groups[1:]
+    return [groups[:1] + inner[part % len(inner) :] + inner[: part % len(inner)] for part in range(parts)]
+
+
+def cube_counts(order, chunks):
+    counts = []
+    for group in order:
+        chunks = chunks >> len(group)
+        counts.append(chunks)
+    return counts
+
+
+def cube_kernel(orders, chunks, extra, value, *refs):
     steps = len(orders[0])
     if extra:
         arrived, out, *results = refs[:6]
@@ -68,54 +76,76 @@
     else:
         out, *scratch = refs
         work = iter(())
-    share = 2
+    share = 3
     kept, sems = scratch[:-1], scratch[-1]
-    chunks = 1 << steps
+    counts = [cube_counts(order, chunks) for order in orders]
 
     def side(bit):
         axis, weight = bit
         return lax.rem(lax.axis_index(axis) // weight, 2)
 
-    def partner(bit):
-        axis, weight = bit
+    def digit(group, flip):
+        total = 0
+        for k, bit in enumerate(group):
+            total = total + (1 - side(bit) if flip >> k & 1 else side(bit)) * (1 << k)
+        return total
+
+    def partner(group, flip):
         place = {name: lax.axis_index(name) for name in ("wide", "narrow")}
-        place[axis] = place[axis] + weight - 2 * weight * side(bit)
+        for k, bit in enumerate(group):
+            if flip >> k & 1:
+                place[bit[0]] = place[bit[0]] + bit[1] - 2 * bit[1] * side(bit)
         return (place["wide"], place["narrow"])
 
-    def copy(source, target, bit, part, step, phase):
-        return pltpu.make_async_remote_copy(
-            src_ref=source, dst_ref=target, send_sem=sems.at[0, phase, part, step], recv_sem=sems.at[1, phase, part, step],
-            device_id=partner(bit), device_id_type=pl.DeviceIdType.MESH,
+    flips = lambda group: range(1, 1 << len(group))
+
+    def copy(source, target, group, flip, part, step, phase):
+        made = pltpu.make_async_remote_copy(
+            src_ref=source, dst_ref=target, send_sem=sems.at[0, phase, part, step, flip - 1],
+            recv_sem=sems.at[1, phase, part, step, flip - 1], device_id=partner(group, flip),
+            device_id_type=pl.DeviceIdType.MESH,
         )
+        made.start()
+        return made
 
     barrier = pltpu.get_barrier_semaphore()
-    for bit in orders[0]:
-        pl.semaphore_signal(barrier, inc=1, device_id=partner(bit), device_id_type=pl.DeviceIdType.MESH)
-    pl.semaphore_wait(barrier, steps)
+    greeted = 0
+    for group in orders[0]:
+        for flip in flips(group):
+            pl.semaphore_signal(barrier, inc=1, device_id=partner(group, flip), device_id_type=pl.DeviceIdType.MESH)
+            greeted += 1
+    pl.semaphore_wait(barrier, greeted)
 
     def held(part, step):
         if step < 0:
             return value.at[pl.ds(part * chunks, chunks)]
-        return kept[part * steps + step]
+        return kept[part * steps + step].at[pl.ds(0, counts[part][step])]
 
     started = []
     flying = {}
 
     def absorb(part, step):
-        count = chunks >> (step + 1)
-        flying[part].wait_recv()
-        spot = held(part, step)
-        spot[...] = spot[...] + held(part, step - 1)[pl.ds(side(orders[part][step]) * count, count)]
+        count = counts[part][step]
+        group = orders[part][step]
+        total = held(part, step - 1)[pl.ds(digit(group, 0) * count, count)]
+        for flip, made in zip(flips(group), flying[part]):
+            made.wait_recv()
+            total = total + kept[part * steps + step][pl.ds((flip - 1) * count, count)]
+        held(part, step)[...] = total
 
     for step in range(steps):
-        count = chunks >> (step + 1)
         for part, order in enumerate(orders):
             if step > 0:
                 absorb(part, step - 1)
-            away = (1 - side(order[step])) * count
-            flying[part] = copy(held(part, step - 1).at[pl.ds(away, count)], held(part, step), order[step], part, step, 0)
-            flying[part].start()
-            started.append(flying[part])
+            group, count = order[step], counts[part][step]
+            flying[part] = [
+                copy(
+                    held(part, step - 1).at[pl.ds(digit(group, flip) * count, count)],
+                    kept[part * steps + step].at[pl.ds((flip - 1) * count, count)], group, flip, part, step, 0,
+                )
+                for flip in flips(group)
+            ]
+            started += flying[part]
         for _ in range(share):
             next(work, None)
     bases = []
@@ -124,25 +154,25 @@
         base = part * chunks
         listed = []
         for step in range(steps):
-            base = base + side(order[step]) * (chunks >> (step + 1))
+            base = base + digit(order[step], 0) * counts[part][step]
             listed.append(base)
         bases.append(listed)
         out[pl.ds(base, 1)] = held(part, steps - 1)[...]
     for step in reversed(range(steps)):
-        count = chunks >> (step + 1)
         for part, order in enumerate(orders):
             if step < steps - 1:
-                flying[part].wait_recv()
-            span = out.at[pl.ds(bases[part][step], count)]
-            flying[part] = copy(span, span, order[step], part, step, 1)
-            flying[part].start()
-            started.append(flying[part])
+                for made in flying[part]:
+                    made.wait_recv()
+            span = out.at[pl.ds(bases[part][step], counts[part][step])]
+            flying[part] = [copy(span, span, order[step], flip, part, step, 1) for flip in flips(order[step])]
+            started += flying[part]
         for _ in range(share):
             next(work, None)
     for _ in work:
         pass
     for part in range(len(orders)):
-        flying[part].wait_recv()
+        for made in flying[part]:
+            made.wait_recv()
     for sent in started:
         sent.wait_send()
 
@@ -155,7 +185,10 @@
     steps = len(orders[0])
     depth = rows // (parts * chunks)
     shape = (parts * chunks, depth, columns)
-    slots = [pltpu.VMEM((chunks >> (step + 1), depth, columns), value.dtype) for _ in orders for step in range(steps)]
+    slots = [
+        pltpu.VMEM((((1 << len(group)) - 1) * count, depth, columns), value.dtype)
+        for order in orders for group, count in zip(order, cube_counts(order, chunks))
+    ]
     extra = () if arrived is None else (arrived,)
     shapes = [jax.ShapeDtypeStruct(shape, value.dtype)]
     if extra:
@@ -163,11 +196,11 @@
         square = jax.ShapeDtypeStruct((2, block // 2, block // 2), f32)
         shapes += [square, square, square, jax.ShapeDtypeStruct((block, block), bf16)]
     summed, *results = pl.pallas_call(
-        functools.partial(cube_kernel, orders, bool(extra)),
+        functools.partial(cube_kernel, orders, chunks, bool(extra)),
         in_specs=[whole_vmem] * (1 + len(extra)),
         out_specs=[whole_vmem] * len(shapes),
         out_shape=shapes,
-        scratch_shapes=slots + [pltpu.SemaphoreType.DMA((2, 2, parts, steps))],
+        scratch_shapes=slots + [pltpu.SemaphoreType.DMA((2, 2, parts, steps, 3))],
         compiler_params=pltpu.CompilerParams(collective_id=number, has_side_effects=True, vmem_limit_bytes=40 << 20),
         name="cube_sum",
     )(value.reshape(shape), *extra)

time: 88.2 us -> 78.4 us (0.89)
  Pallas kernels: 83.5 us -> 74.4 us
    pallas_call x2, Pallas kernels: 65.6 us -> 56.6 us  [cube_sum(): pl.pallas_call(functools.partial(cube_kernel, orders, chunks, bool(extra)...]
where the time goes in v4:
time: 78.4 us; the launch traced here: 77.5 us
  Pallas kernels  74.4 us (95%)
  local copies, waits for them, and re-layouts  2.99 us (4%)
    pallas_call x2, Pallas kernels, cube_sum(): pl.pallas_call(functools.partial(cube_kernel, orders, chunks, bool(extra)...  56.6 us
    pallas_call x1, Pallas kernels, local_terms(): pl.pallas_call(terms_kernel, grid=(count // tile,), in_specs=[still(arriv...  8.01 us
    pallas_call x1, Pallas kernels, gather_own(): pl.pallas_call(gather_kernel, grid=(count // tile,), in_specs=[whole_smem...  7.35 us
    unnamed x18, local copies, waits for them, and re-layouts  2.99 us
    pallas_call x1, Pallas kernels, finish(): pl.pallas_call(finish_kernel, grid=(count // tile,), in_specs=[whole_smem...  2.46 us

profile of v4, /device:TPU:0, one launch (start us, length us, event | category | flops | bytes accessed | tf_op | source)
XLA Modules:
  0.0 77.5 jit_solution(17072243773327941758)
XLA Ops:
  0.0 0.0 copy-start
  0.0 7.3 %gather_own.1 = (bf16[1024,512]{1,0:T(8,128)(2,1)}, f32[1024,128]{1,0:T(8,128)}, bf16[4096,128]{1,0:T(8,128)(2,1)}, bf16[4096,128]{1,0:T(8,128)(2,1)}, f32[1,4096]{1,0:T(1,128)}) custom-call(s32[2]{0:T(128)} %owners.3, s32[2,512]{1,0:T(2,128)} %listed.3, bf16[4096,512]{1,0:T(8,128)(2,1)} %feats.3, f32[4096,128]{1,0:T(8,128)} %coefs.3, bf16[4096,128]{1,0:T(8,128)(2,1)} %targs.1), custom_call_target="tpu_custom_call" | custom-call | tf_op jit(solution)/shard_map/gather_own/pallas_call | solution.py:276
  7.3 0.0 copy-start.2
  7.4 1.2 %copy-done.2 = bf16[1024,512]{1,0:T(8,128)(2,1)S(1)} copy-done((bf16[1024,512]{1,0:T(8,128)(2,1)S(1)}, bf16[1024,512]{1,0:T(8,128)(2,1)}, u32[]{:S(2)}) %copy-start.2) | copy-done | bytes 1048600
  8.6 0.0 copy-start.3
  8.6 0.0 copy-start.4
  8.6 33.2 %cube_sum.2 = bf16[128,8,512]{2,1,0:T(8,128)(2,1)S(1)} custom-call(bf16[128,8,512]{2,1,0:T(8,128)(2,1)S(1)} %bitcast.7), custom_call_target="tpu_custom_call" | custom-call | tf_op jit(solution)/shard_map/cube_sum/pallas_call | solution.py:198
  41.8 0.0 copy-done
  41.8 0.0 copy-done.3
  41.8 0.0 copy-done.4
  41.8 0.0 copy-start.5
  41.8 1.0 %copy-done.5 = f32[1024,128]{1,0:T(8,128)S(1)} copy-done((f32[1024,128]{1,0:T(8,128)S(1)}, f32[1024,128]{1,0:T(8,128)}, u32[]{:S(2)}) %copy-start.5) | copy-done | bytes 524312
  42.9 0.0 copy-start.7
  42.9 0.7 copy-done.7
  43.6 0.0 copy-start.1
  43.6 0.0 copy-start.6
  43.6 0.0 copy-start.8
  43.6 8.0 %local_terms.1 = f32[1024,128]{1,0:T(8,128)S(1)} custom-call(bf16[1024,512]{1,0:T(8,128)(2,1)S(1)} %bitcast.4, bf16[4096,512]{1,0:T(8,128)(2,1)S(1)} %copy-done, f32[1,4096]{1,0:T(1,128)S(1)} %copy-done.7, bf16[4096,128]{1,0:T(8,128)(2,1)S(1)} %copy-done.3, bf16[4096,128]{1,0:T(8,128)(2,1)S(1)} %copy-done.4, f32[1024,128]{1,0:T(8,128)S(1)} %copy-done.5), custom_call_target="tpu_custom_call" | custom-call | tf_op jit(solution)/shard_map/local_terms/pallas_call | solution.py:322
  51.6 23.4 %cube_sum.3 = (f32[128,8,128]{2,1,0:T(8,128)S(1)}, f32[2,256,256]{2,1,0:T(8,128)S(1)}, f32[2,256,256]{2,1,0:T(8,128)S(1)}, f32[2,256,256]{2,1,0:T(8,128)S(1)}, bf16[512,512]{1,0:T(8,128)(2,1)S(1)}) custom-call(f32[128,8,128]{2,1,0:T(8,128)S(1)} %bitcast.6, bf16[1024,512]{1,0:T(8,128)(2,1)S(1)} %bitcast.5), custom_call_target="tpu_custom_call" | custom-call | tf_op jit(solution)/shard_map/cube_sum/pallas_call | solution.py:198
  75.0 0.0 copy-done.1
  75.0 0.0 copy-done.6
  75.1 0.0 copy-done.8
  75.1 2.5 %finish.1 = f32[4096,128]{1,0:T(8,128)} custom-call(s32[2]{0:T(128)S(1)} %copy-done.8, s32[2,512]{1,0:T(2,128)S(1)} %copy-done.6, f32[4096,128]{1,0:T(8,128)S(1)} %copy-done.1, f32[1024,128]{1,0:T(8,128)S(1)} %bitcast.8, f32[2,256,256]{2,1,0:T(8,128)S(1)} %get-tuple-element.21.first_inv, f32[2,256,256]{2,1,0:T(8,128)S(1)} %get-tuple-element.22.cross, ...), custom_call_target="tpu_custom_call" | custom-call | tf_op jit(solution)/shard_map/finish/pallas_call | solution.py:442
Async XLA Ops:
  0.0 41.8 %copy-start = (bf16[4096,512]{1,0:T(8,128)(2,1)S(1)}, bf16[4096,512]{1,0:T(8,128)(2,1)}, u32[]{:S(2)}) copy-start(bf16[4096,512]{1,0:T(8,128)(2,1)} %feats.3) | copy-start | bytes 12582916
  7.3 1.2 %copy-start.2 = (bf16[1024,512]{1,0:T(8,128)(2,1)S(1)}, bf16[1024,512]{1,0:T(8,128)(2,1)}, u32[]{:S(2)}) copy-start(bf16[1024,512]{1,0:T(8,128)(2,1)} %get-tuple-element.15) | copy-start | bytes 3145732
  8.6 33.2 %copy-start.3 = (bf16[4096,128]{1,0:T(8,128)(2,1)S(1)}, bf16[4096,128]{1,0:T(8,128)(2,1)}, u32[]{:S(2)}) copy-start(bf16[4096,128]{1,0:T(8,128)(2,1)} %get-tuple-element.17.mask0) | copy-start | bytes 3145732
  8.6 33.2 %copy-start.4 = (bf16[4096,128]{1,0:T(8,128)(2,1)S(1)}, bf16[4096,128]{1,0:T(8,128)(2,1)}, u32[]{:S(2)}) copy-start(bf16[4096,128]{1,0:T(8,128)(2,1)} %get-tuple-element.18.mask1) | copy-start | bytes 3145732
  41.8 1.0 %copy-start.5 = (f32[1024,128]{1,0:T(8,128)S(1)}, f32[1024,128]{1,0:T(8,128)}, u32[]{:S(2)}) copy-start(f32[1024,128]{1,0:T(8,128)} %get-tuple-element.19.own) | copy-start | bytes 1572868
  42.9 0.7 copy-start.7
  43.6 31.4 %copy-start.1 = (f32[4096,128]{1,0:T(8,128)S(1)}, f32[4096,128]{1,0:T(8,128)}, u32[]{:S(2)}) copy-start(f32[4096,128]{1,0:T(8,128)} %coefs.3) | copy-start | bytes 6291460
  43.6 31.5 %copy-start.6 = (s32[2,512]{1,0:T(2,128)S(1)}, s32[2,512]{1,0:T(2,128)}, u32[]{:S(2)}) copy-start(s32[2,512]{1,0:T(2,128)} %listed.3) | copy-start | bytes 12292
  43.6 31.5 %copy-start.8 = (s32[2]{0:T(128)S(1)}, s32[2]{0:T(128)}, u32[]{:S(2)}) copy-start(s32[2]{0:T(128)} %owners.3) | copy-start | bytes 28
